TPU v7x, 256 devices: a whole 4x4x8 slice. The times are simulated.
256 devices in a mesh: aux: 8 (over x, core), orb: 32 (over z, y).
Axes of the slice: x: 4, y: 4, z: 8, core: 2. Of those that a mesh axis runs over, the one named last changes fastest.
Arguments:
- three_center: float32 [32, 32, 128, 1024], P('aux', 'orb'), may hold values from -6 to 6
- tile_lists: int32 [2, 32, 8, 8], P(None, 'aux'), may hold values from -1 to 7, as said below
- occ_density: float32 [2, 1024, 1024], P(None, 'orb', 'aux'), may hold values from -0.1875 to 0.1875
- vir_density: float32 [2, 1024, 1024], P(None, 'orb', 'aux'), may hold values from -0.1875 to 0.1875
Outputs:
- coupled: float32 [2, 32, 32, 1024, 128], P(None, 'aux', 'orb')
Inputs may be any that keep to these rules, and one draw needn't show every extreme that they name: Row m of tile_lists[t, j] names distinct orbital blocks in rising order, block m always among them, and -1 in the remaining places; it names between 2 and 8 blocks, and for every t and j one row names all 8 and another exactly 2.
All inputs are finite; a program needn't handle non-finite values.
Results may differ from a plain program's by a relative error of at most 0.0003.
Values sent between devices are 32-bit elements; how exact they have to be, the bound alone decides.
A program may use at most 64 MiB of HBM per device.

v0:
```python
import jax
import jax.numpy as jnp
from jax import lax
from jax.sharding import PartitionSpec as P


def listed_mask(tile_lists, part_index, block_index):
    block_table = lax.dynamic_index_in_dim(tile_lists, part_index, 1, keepdims=False)
    listed_row = lax.dynamic_index_in_dim(block_table, block_index, 1, keepdims=False)
    block_count = tile_lists.shape[3]
    block_ids = jnp.arange(block_count, dtype=jnp.int32)
    matches = listed_row[:, :, None] == block_ids[None, None, :]
    return jnp.sum(matches.astype(jnp.float32), axis=1)


def masked_rows(integrals, listed_now):
    aux_count, block_size, orbitals = integrals.shape
    block_count = orbitals // block_size
    viewed = integrals.reshape(aux_count, block_size, block_count, block_size)
    masked = viewed[None] * listed_now[:, None, None, :, None]
    return masked.reshape(listed_now.shape[0], aux_count * block_size, orbitals)


def make_adder(masked, density_rows):
    return jnp.einsum("tar,trl->tal", masked, density_rows, precision=lax.Precision.HIGHEST)


def make_applier(column_data, density_rows):
    return jnp.einsum("tsk,takl->tasl", density_rows, column_data, precision=lax.Precision.HIGHEST)


def outgoing(product, listed_now, aux_count, block_size, block_count, split_count):
    time_count = product.shape[0]
    aux_share = aux_count // split_count
    pruned = product.reshape(time_count, aux_count, block_size, block_count, block_size)
    pruned = pruned * listed_now[:, None, None, :, None]
    split_view = pruned.reshape(
        time_count, split_count, aux_share, block_size, block_count, block_size
    )
    ordered = split_view.transpose(4, 1, 0, 2, 3, 5)
    return ordered.reshape(block_count * split_count, time_count, aux_share, block_size, block_size)


def make_arrange(block_count, split_count):

    def arrange(received):
        unit_count, time_count, item_count, row_count, col_count = received.shape
        grouped = received.reshape(
            block_count, split_count, time_count, item_count, row_count, col_count
        )
        reordered = grouped.transpose(2, 1, 3, 0, 4, 5)
        return reordered.reshape(
            time_count, split_count, item_count, block_count * row_count, col_count
        )

    return arrange


def local(three_center, tile_lists, occ_density, vir_density):
    aux_count = three_center.shape[0]
    block_size = three_center.shape[2]
    orbitals = three_center.shape[3]
    block_count = orbitals // block_size
    owners = lax.axis_size("orb")
    split_count = owners // block_count
    owner_unit = lax.axis_index("orb")
    block_index = owner_unit // split_count
    part_index = owner_unit % split_count
    listed = listed_mask(tile_lists, part_index, block_index)
    integrals = three_center[:, 0]
    arrange = make_arrange(block_count, split_count)
    occ_cols, vir_cols = (
        lax.all_gather(occ_density, "aux", axis=2, tiled=True),
        lax.all_gather(vir_density, "aux", axis=2, tiled=True),
    )
    results = []
    for moment in range(occ_cols.shape[0]):
        listed_now = listed[moment : moment + 1]
        masked = masked_rows(integrals, listed_now)
        product = make_adder(
            masked, lax.all_gather(occ_cols[moment : moment + 1], "orb", axis=1, tiled=True)
        )
        sending = outgoing(product, listed_now, aux_count, block_size, block_count, split_count)
        column_data = arrange(
            lax.all_to_all(sending, "orb", split_axis=0, concat_axis=0, tiled=True)
        )
        column_data = column_data.reshape(1, aux_count, orbitals, block_size)
        results.append(
            make_applier(
                column_data,
                lax.all_gather(vir_cols[moment : moment + 1], "orb", axis=1, tiled=True),
            )
        )
    coupled = jnp.concatenate(results, axis=0)
    return coupled[:, :, None]


def solution(mesh):
    in_specs = (
        P("aux", "orb", None, None),
        P(None, "aux", None, None),
        P(None, "orb", "aux"),
        P(None, "orb", "aux"),
    )
    out_specs = P(None, "aux", "orb", None, None)
    return jax.shard_map(local, mesh=mesh, in_specs=in_specs, out_specs=out_specs, check_vma=False)
```

profile of v0, /device:TPU:57, one launch (start us, length us, event | category | flops | bytes accessed | tf_op | source)
XLA Modules:
  0.0 395.7 jit_solution(4999827515869615526)
XLA Ops:
  6.5 14.0 %all_gather.18 = f32[2,32,1024]{2,1,0:T(8,128)S(1)} all-gather(f32[2,32,128]{2,1,0:T(8,128)} %param.6), channel_id=1, replica_groups=mesh['aux'=8,'orb'=32] {'aux'}, dimensions={2}, use_global_device_ids=true | all-gather | bytes 294912 | tf_op jit(solution)/shard_map/all_gather | solution.py:73
  20.6 0.7 fusion.23
  21.3 0.0 all-gather.5.cloned.1.call-start
  21.4 0.7 all-gather.5.cloned.1.call-update
  22.1 0.0 all-gather.7.cloned.1.call-start
  22.1 13.1 %all_gather.20 = f32[2,32,1024]{2,1,0:T(8,128)S(1)} all-gather(f32[2,32,128]{2,1,0:T(8,128)} %param.7), channel_id=1, replica_groups=mesh['aux'=8,'orb'=32] {'aux'}, dimensions={2}, use_global_device_ids=true | all-gather | bytes 294912 | tf_op jit(solution)/shard_map/all_gather | solution.py:74
  35.2 0.7 fusion.22
  36.0 0.1 convert_reduce_fusion
  36.1 0.1 broadcast_bitcast_fusion
  36.2 62.4 %all-gather.9.cloned.1.call-done = f32[1,1024,1024]{2,1,0:T(8,128)} async-done(((f32[1,32,1024]{2,1,0:T(8,128)}), f32[1,1024,1024]{2,1,0:T(8,128)}) %all-gather.9.cloned.1.call-update) | async-done | bytes 4194320 | tf_op jit(solution)/shard_map/all_gather | solution.py:81
  98.5 5.3 %copy.28 = f32[1024,1024]{1,0:T(8,128)} copy(f32[1024,1024]{0,1:T(8,128)} %bitcast.95) | data formatting | bytes 8388608 | tf_op jit(solution)/shard_map/tar,trl->tal/dot_general | solution.py:25
  103.9 9.4 %multiply_bitcast_fusion = f32[8,4,1,1,128,128]{5,4,0,1,3,2:T(8,128)S(1)} fusion(f32[8,128,1024,1]{2,1,0,3:T(8,128)} %bitcast.97, f32[4,1,128,1024]{3,2,1,0:T(8,128)} %param.4, f32[8]{0:T(128)S(1)} %get-tuple-element.10, f32[1024]{0:T(1024)S(1)} %get-tuple-element.11), kind=kOutput, calls=%fused_computation.9 | convolution fusion | flops 6443499520 | bytes 8392736 | tf_op jit(solution)/shard_map/tar,trl->tal/dot_general | solution.py:25
  113.3 1.5 copy.29
  114.8 8.3 %all-to-all-start.1 = ((f32[32,1,1,128,128]{4,3,2,1,0:T(8,128)}), f32[32,1,1,128,128]{4,3,2,1,0:T(8,128)S(1)}, u32[]{:S(2)}, u32[]{:S(2)}) async-start(f32[32,1,1,128,128]{4,3,2,1,0:T(8,128)} %bitcast.92), calls=%async_computation.1 | async-start | bytes 4194304 | tf_op jit(solution)/shard_map/all_to_all | solution.py:85
  123.1 0.0 all-gather.11.cloned.1.call-start
  123.2 0.5 all-gather.11.cloned.1.call-update
  123.7 72.4 %all-gather.5.cloned.1.call-done = f32[1,1024,1024]{2,1,0:T(8,128)} async-done(((f32[1,32,1024]{2,1,0:T(8,128)}), f32[1,1024,1024]{2,1,0:T(8,128)}) %all-gather.5.cloned.1.call-update) | async-done | bytes 4194320 | tf_op jit(solution)/shard_map/all_gather | solution.py:81
  196.1 5.3 %copy.24 = f32[1024,1024]{1,0:T(8,128)} copy(f32[1024,1024]{0,1:T(8,128)} %bitcast.94) | data formatting | bytes 8388608 | tf_op jit(solution)/shard_map/tar,trl->tal/dot_general | solution.py:25
  201.4 9.4 %multiply_bitcast_fusion.1 = f32[8,4,1,1,128,128]{5,4,0,1,3,2:T(8,128)S(1)} fusion(f32[8,128,1024,1]{2,1,0,3:T(8,128)} %bitcast.96, f32[4,1,128,1024]{3,2,1,0:T(8,128)} %param.4, f32[8]{0:T(128)S(1)} %get-tuple-element.9, f32[1024]{0:T(1024)S(1)} %get-tuple-element.12), kind=kOutput, calls=%fused_computation.11 | convolution fusion | flops 6443499520 | bytes 8392736 | tf_op jit(solution)/shard_map/tar,trl->tal/dot_general | solution.py:25
  210.9 1.5 copy.25
  212.4 7.5 %all-to-all-start = ((f32[32,1,1,128,128]{4,3,2,1,0:T(8,128)}), f32[32,1,1,128,128]{4,3,2,1,0:T(8,128)}, u32[]{:S(2)}, u32[]{:S(2)}) async-start(f32[32,1,1,128,128]{4,3,2,1,0:T(8,128)} %bitcast.93), calls=%async_computation | async-start | bytes 4194304 | tf_op jit(solution)/shard_map/all_to_all | solution.py:85
  219.9 1.8 copy.31
  221.7 2.8 reshape.106
  224.5 53.7 %all-to-all-done = f32[32,1,1,128,128]{4,3,2,1,0:T(8,128)} async-done(((f32[32,1,1,128,128]{4,3,2,1,0:T(8,128)}), f32[32,1,1,128,128]{4,3,2,1,0:T(8,128)}, u32[]{:S(2)}, u32[]{:S(2)}) %all-to-all-start) | async-done | bytes 2097184 | tf_op jit(solution)/shard_map/all_to_all | solution.py:85
  278.2 2.0 copy.27
  280.2 1.5 reshape.100
  281.7 11.0 %all-gather.7.cloned.1.call-done = f32[1,1024,1024]{2,1,0:T(8,128)} async-done(((f32[1,32,1024]{2,1,0:T(8,128)}), f32[1,1024,1024]{2,1,0:T(8,128)}) %all-gather.7.cloned.1.call-update) | async-done | bytes 4194320 | tf_op jit(solution)/shard_map/all_gather | solution.py:91
  292.7 10.3 %fusion.14 = f32[1,4,1024,128]{2,3,1,0:T(8,128)} fusion(f32[4,1024,128]{1,2,0:T(8,128)} %reshape.100, f32[1,1024,1024]{2,1,0:T(8,128)} %all-gather.7.cloned.1.call-done), kind=kOutput, calls=%fused_computation.13 | convolution fusion | flops 6442450944 | bytes 8388608 | tf_op jit(solution)/shard_map/tsk,takl->tasl/dot_general | solution.py:29
  303.0 69.4 %all-gather.11.cloned.1.call-done = f32[1,1024,1024]{2,1,0:T(8,128)} async-done(((f32[1,32,1024]{2,1,0:T(8,128)}), f32[1,1024,1024]{2,1,0:T(8,128)}) %all-gather.11.cloned.1.call-update) | async-done | bytes 4194320 | tf_op jit(solution)/shard_map/all_gather | solution.py:91
  372.4 9.2 %fusion.17 = f32[1,4,1024,128]{2,3,1,0:T(8,128)S(1)} fusion(f32[4,1024,128]{1,2,0:T(8,128)S(1)} %copy-done.1, f32[1,1024,1024]{2,1,0:T(8,128)} %all-gather.11.cloned.1.call-done), kind=kOutput, calls=%fused_computation.14 | convolution fusion | flops 6442450944 | bytes 8388608 | tf_op jit(solution)/shard_map/tsk,takl->tasl/dot_general | solution.py:29
  381.6 2.3 maximum_bitcast_fusion
  383.9 5.3 %copy.32 = f32[2,4,1,1024,128]{4,3,2,1,0:T(8,128)} copy(f32[2,4,1,1024,128]{3,4,1,0,2:T(8,128)} %maximum_bitcast_fusion) | data formatting | bytes 8388608 | tf_op jit(solution)/shard_map/broadcast_in_dim | solution.py:95
  (12 shorter events, 0.1 us)
Async XLA Ops:
  6.5 29.4 %copy-start = (s32[2,4,8,8]{3,2,1,0:T(8,128)S(1)}, s32[2,4,8,8]{3,2,1,0:T(8,128)}, u32[]{:S(2)}) copy-start(s32[2,4,8,8]{3,2,1,0:T(8,128)} %param.5) | copy-start | bytes 6148
  6.5 92.0 %all-gather.9.cloned.1.call-start = ((), (), s32[]{:S(2)}) async-start(), calls=%async_computation.4 | async-start | bytes 4325376 | tf_op jit(solution)/shard_map/all_gather | solution.py:81
  21.3 174.8 %all-gather.5.cloned.1.call-start = ((), (), s32[]{:S(2)}) async-start(), calls=%async_computation.2 | async-start | bytes 4325376 | tf_op jit(solution)/shard_map/all_gather | solution.py:81
  22.1 270.6 %all-gather.7.cloned.1.call-start = ((), (), s32[]{:S(2)}) async-start(), calls=%async_computation.3 | async-start | bytes 4325376 | tf_op jit(solution)/shard_map/all_gather | solution.py:91
  114.8 97.6 %all-to-all-start.1 = ((f32[32,1,1,128,128]{4,3,2,1,0:T(8,128)}), f32[32,1,1,128,128]{4,3,2,1,0:T(8,128)S(1)}, u32[]{:S(2)}, u32[]{:S(2)}) async-start(f32[32,1,1,128,128]{4,3,2,1,0:T(8,128)} %bitcast.92), calls=%async_computation.1 | async-start | bytes 4194304 | tf_op jit(solution)/shard_map/all_to_all | solution.py:85
  123.1 249.3 %all-gather.11.cloned.1.call-start = ((), (), s32[]{:S(2)}) async-start(), calls=%async_computation.5 | async-start | bytes 4325376 | tf_op jit(solution)/shard_map/all_gather | solution.py:91
  212.4 65.8 %all-to-all-start = ((f32[32,1,1,128,128]{4,3,2,1,0:T(8,128)}), f32[32,1,1,128,128]{4,3,2,1,0:T(8,128)}, u32[]{:S(2)}, u32[]{:S(2)}) async-start(f32[32,1,1,128,128]{4,3,2,1,0:T(8,128)} %bitcast.93), calls=%async_computation | async-start | bytes 4194304 | tf_op jit(solution)/shard_map/all_to_all | solution.py:85
  281.7 90.7 %copy-start.1 = (f32[4,1024,128]{1,2,0:T(8,128)S(1)}, f32[4,1024,128]{1,2,0:T(8,128)}, u32[]{:S(2)}) copy-start(f32[4,1024,128]{1,2,0:T(8,128)} %reshape.106) | copy-start | bytes 6291460
  372.4 9.2 %copy-start.2 = (f32[1,4,1024,128]{2,3,1,0:T(8,128)S(1)}, f32[1,4,1024,128]{2,3,1,0:T(8,128)}, u32[]{:S(2)}) copy-start(f32[1,4,1024,128]{2,3,1,0:T(8,128)} %fusion.14) | copy-start | bytes 6291460
Sparse Core Ops, SparseCore 0:
  21.4 77.0 all-gather.8
  101.1 94.9 all-gather.4
  198.7 93.9 all-gather.6
  295.1 77.2 all-gather.10
where the time goes:
time: 403 us; the launch traced here: 396 us
  waiting for transfers between devices  270 us (67%)
  matrix products  38.4 us (10%)
  local copies, waits for them, and re-layouts  28.7 us (7%)
  blocking collectives  27.1 us (7%)
  starting transfers between devices  16 us (4%)
  between operations  13.2 us (3%)
    all_gather x2, waiting for transfers between devices, local(): lax.all_gather(occ_cols[moment:moment + 1], 'orb', axis=1, tiled=True)  135 us
    all_gather x2, waiting for transfers between devices, local(): lax.all_gather(vir_cols[moment:moment + 1], 'orb', axis=1, tiled=True)  80.4 us
    all_to_all x2, waiting for transfers between devices, local(): lax.all_to_all(sending, 'orb', split_axis=0, concat_axis=0, tiled=True)  53.7 us
    dot_general x2, matrix products, make_applier(): jnp.einsum('tsk,takl->tasl', density_rows, column_data, precision=lax.Pre...  19.5 us
    dot_general x2, matrix products, make_adder(): jnp.einsum('tar,trl->tal', masked, density_rows, precision=lax.Precision....  18.9 us
    all_to_all x2, starting transfers between devices, local(): lax.all_to_all(sending, 'orb', split_axis=0, concat_axis=0, tiled=True)  15.9 us
    all_gather x1, blocking collectives, local(): lax.all_gather(occ_density, 'aux', axis=2, tiled=True)  14 us
    all_gather x1, blocking collectives, local(): lax.all_gather(vir_density, 'aux', axis=2, tiled=True)  13.1 us
  transfers between devices with their start and end apart: 6, of which 5 were waited for; matrix products, arithmetic and copies ran while one was open for 13% of the time, Pallas kernels for 0%

commit v1 on v0

v1 whole, which is shorter than its diff:
```python
import functools

import jax
import jax.numpy as jnp
from jax import lax
from jax.experimental import pallas as pl
from jax.experimental.pallas import tpu as pltpu
from jax.sharding import PartitionSpec as P

MESH = pl.DeviceIdType.MESH
NX, NC, NZ, NY = 4, 2, 8, 4
BLK = 128
OCC, VIR = 0, 1


def listed_mask(tile_lists, part_index, block_index):
    block_table = lax.dynamic_index_in_dim(tile_lists, part_index, 1, keepdims=False)
    listed_row = lax.dynamic_index_in_dim(block_table, block_index, 1, keepdims=False)
    block_count = tile_lists.shape[3]
    block_ids = jnp.arange(block_count, dtype=jnp.int32)
    matches = listed_row[:, :, None] == block_ids[None, None, :]
    return jnp.sum(matches.astype(jnp.float32), axis=1)


def split(value):
    high = value.astype(jnp.bfloat16)
    return high, (value - high.astype(jnp.float32)).astype(jnp.bfloat16)


def three_pass(a_high, a_low, b_high, b_low):
    dot = functools.partial(jnp.dot, preferred_element_type=jnp.float32)
    return dot(a_high, b_high) + dot(a_high, b_low) + dot(a_low, b_high)


def kernel(
    mask, three_center, occ_in, vir_in, coupled,
    rows, int_high, int_low, occ, vir, sending, received,
    one_high, one_low, two_high, two_low,
    rows_sem, own_sem, zs, zr, ys, yr, xs, xr, rs, rr, cs, cr, out_sem, in_sem,
):
    aux, orb = lax.axis_index("aux"), lax.axis_index("orb")
    x, c, z, y = lax.div(aux, NC), lax.rem(aux, NC), lax.div(orb, NY), lax.rem(orb, NY)
    pair = lax.div(z, 2)
    inputs, full = (occ_in, vir_in), (occ, vir)

    def device(at_x, at_c, at_z, at_y):
        return (at_x * NC + at_c, at_z * NY + at_y)

    def along_x(step):
        return lax.rem(x + step + NX, NX)

    def along_z(step):
        return lax.rem(z + step, NZ)

    def along_y(step):
        return lax.rem(y + step, NY)

    def send(source, target, send_sem, recv_sem, to):
        pltpu.make_async_remote_copy(
            src_ref=source, dst_ref=target, send_sem=send_sem, recv_sem=recv_sem,
            device_id=to, device_id_type=MESH,
        ).start()

    def wait(ref, sem):
        pltpu.make_async_copy(ref, ref, sem).wait()

    def own_copy(g, t):
        return pltpu.make_async_copy(inputs[g].at[t], full[g].at[t, aux, z, y], own_sem.at[g, t])

    rows_copy = pltpu.make_async_copy(three_center.at[:, 0], rows, rows_sem)
    for g in (OCC, VIR):
        for t in range(2):
            own_copy(g, t).start()
    rows_copy.start()

    barrier = pltpu.get_barrier_semaphore()
    peers = [device(x, c, along_z(d), y) for d in range(1, NZ)]
    peers += [device(x, c, z, along_y(d)) for d in range(1, NY)]
    peers += [device(along_x(d), c, z, y) for d in (1, -1)]
    peers += [device(x, 1 - c, z, y)]
    for peer in peers:
        pl.semaphore_signal(barrier, inc=1, device_id=peer, device_id_type=MESH)
    pl.semaphore_wait(barrier, len(peers))

    def z_start(g, t):
        own_copy(g, t).wait()
        piece = full[g].at[t, aux, z, y]
        for d in (4, 3, 5, 2, 6, 1, 7):
            send(piece, piece, zs.at[g, t], zr.at[g, t], device(x, c, along_z(d), y))

    def z_wait(g, t):
        wait(full[g].at[t, aux, pl.ds(0, NZ - 1), y], zr.at[g, t])

    def y_start(g, t):
        piece = full[g].at[t, aux, :, y]
        for d in (2, 1, 3):
            send(piece, piece, ys.at[g, t], yr.at[g, t], device(x, c, z, along_y(d)))

    def y_wait(g, t):
        wait(full[g].at[t, aux, :, pl.ds(0, NY - 1)], yr.at[g, t])

    def column(g, t, at_x):
        return full[g].at[t, at_x * NC + c]

    def core_start(g, t, at_x):
        piece = column(g, t, at_x)
        send(piece, piece, cs.at[g, t], cr.at[g, t], device(x, 1 - c, z, y))

    def core_wait(g, t):
        wait(full[g].at[t, pl.ds(0, NX)], cr.at[g, t])

    def x_start(g, t):
        piece = column(g, t, x)
        send(piece, piece, xs.at[g, t], xr.at[g, t, 0], device(along_x(1), c, z, y))
        send(piece, piece, xs.at[g, t], xr.at[g, t, 1], device(along_x(-1), c, z, y))
        core_start(g, t, x)

    def x_relay(g, t):
        for side, (origin, onward) in enumerate(((-1, 1), (1, -1))):
            at_x = along_x(origin)
            wait(column(g, t, at_x), xr.at[g, t, side])
            piece = full[g].at[t, at_x * NC + c, pl.ds(side * (NZ // 2), NZ // 2)]
            send(piece, piece, rs.at[g, t], rr.at[g, t], device(along_x(onward), c, z, y))
            core_start(g, t, at_x)

    def x_finish(g, t):
        at_x = along_x(2)
        wait(column(g, t, at_x), rr.at[g, t])
        core_start(g, t, at_x)

    def half_stage(t):
        def unit(k, carry):
            p = lax.rem(pair + 2 + k, NX)
            for h in range(2):
                for n in range(NZ):
                    block = occ[t, 2 * p + h, n].reshape(BLK, BLK)
                    block = block * mask[pl.ds(t * NZ + n, 1), :]
                    high, low = split(block)
                    one_high[pl.ds(n * BLK, BLK), pl.ds(h * BLK, BLK)] = high
                    one_low[pl.ds(n * BLK, BLK), pl.ds(h * BLK, BLK)] = low
            product = three_pass(int_high[...], int_low[...], one_high[...], one_low[...])
            for h in range(2):
                keep = mask[pl.ds(t * NZ + 2 * p + h, 1), :]
                for r in range(NY):
                    part = product[r * BLK : (r + 1) * BLK, h * BLK : (h + 1) * BLK]
                    sending[t, 2 * p + h, r] = part * keep
            for h in range(2):
                to_z = 2 * p + h
                for r in range(NY):
                    own = jnp.logical_and(to_z == z, y == r)
                    source = sending.at[t, to_z, r]
                    target = received.at[t, z, y]
                    arrived = in_sem.at[t, pair]

                    @pl.when(own)
                    def _():
                        pltpu.make_async_copy(source, target, arrived).start()

                    @pl.when(jnp.logical_not(own))
                    def _():
                        send(source, target, out_sem.at[t], arrived, device(x, c, to_z, r))

            return carry

        lax.fori_loop(0, NX, unit, 0)

    def full_stage(t):
        def unit(k, carry):
            p = lax.rem(pair + 2 - k + NX, NX)
            wait(received.at[t, pl.ds(2 * p, 2)], in_sem.at[t, p])
            for h in range(2):
                for q in range(NY):
                    high, low = split(received[t, 2 * p + h, q])
                    two_high[pl.ds(h * BLK, BLK), pl.ds(q * BLK, BLK)] = high
                    two_low[pl.ds(h * BLK, BLK), pl.ds(q * BLK, BLK)] = low

            def tile(s, inner):
                halves = [
                    split(vir[t, 2 * p + h, pl.ds(2 * s, 2)].reshape(2 * BLK, BLK))
                    for h in range(2)
                ]
                high = jnp.concatenate([halves[0][0], halves[1][0]], axis=1)
                low = jnp.concatenate([halves[0][1], halves[1][1]], axis=1)
                product = three_pass(high, low, two_high[...], two_low[...])
                for q in range(NY):
                    at = (t, q, pl.ds(s * 2 * BLK, 2 * BLK), slice(None))
                    coupled[at] += product[:, q * BLK : (q + 1) * BLK]
                return inner

            lax.fori_loop(0, NZ // 2, tile, 0)
            return carry

        lax.fori_loop(0, NX, unit, 0)

    z_start(OCC, 0)
    rows_copy.wait()
    for r in range(NY):
        high, low = split(rows[r])
        int_high[pl.ds(r * BLK, BLK), :] = high
        int_low[pl.ds(r * BLK, BLK), :] = low

    z_wait(OCC, 0)
    y_start(OCC, 0)
    z_start(OCC, 1)
    y_wait(OCC, 0)
    x_start(OCC, 0)
    z_wait(OCC, 1)
    y_start(OCC, 1)
    z_start(VIR, 0)
    z_start(VIR, 1)
    coupled[...] = jnp.zeros_like(coupled)
    x_relay(OCC, 0)
    y_wait(OCC, 1)
    x_start(OCC, 1)
    x_finish(OCC, 0)
    z_wait(VIR, 0)
    y_start(VIR, 0)
    z_wait(VIR, 1)
    y_start(VIR, 1)
    core_wait(OCC, 0)
    half_stage(0)
    x_relay(OCC, 1)
    y_wait(VIR, 0)
    x_start(VIR, 0)
    x_finish(OCC, 1)
    core_wait(OCC, 1)
    half_stage(1)
    x_relay(VIR, 0)
    y_wait(VIR, 1)
    x_start(VIR, 1)
    x_finish(VIR, 0)
    core_wait(VIR, 0)
    x_relay(VIR, 1)
    x_finish(VIR, 1)
    core_wait(VIR, 1)
    full_stage(0)
    full_stage(1)

    for g in (OCC, VIR):
        for t in range(2):
            wait(full[g].at[t, aux, pl.ds(0, NZ - 1), y], zs.at[g, t])
            wait(full[g].at[t, aux, :, pl.ds(0, NY - 1)], ys.at[g, t])
            wait(full[g].at[t, pl.ds(0, 2)], xs.at[g, t])
            wait(full[g].at[t, 0], rs.at[g, t])
            wait(full[g].at[t, pl.ds(0, NX)], cs.at[g, t])
    for t in range(2):
        wait(sending.at[t, pl.ds(0, NZ - 1)], out_sem.at[t])
        wait(sending.at[t, 0, pl.ds(0, NY - 1)], out_sem.at[t])


def local(three_center, tile_lists, occ_density, vir_density):
    owner_unit = lax.axis_index("orb")
    listed = listed_mask(tile_lists, owner_unit % NY, owner_unit // NY)
    times, blocks = listed.shape
    mask = jnp.broadcast_to(listed.reshape(times * blocks, 1), (times * blocks, BLK))
    orbitals = three_center.shape[3]
    dma = pltpu.SemaphoreType.DMA
    coupled = pl.pallas_call(
        kernel,
        out_shape=jax.ShapeDtypeStruct((times, NY, orbitals, BLK), jnp.float32),
        in_specs=[pl.BlockSpec(memory_space=pltpu.VMEM)]
        + [pl.BlockSpec(memory_space=pl.ANY)] * 3,
        out_specs=pl.BlockSpec(memory_space=pltpu.VMEM),
        scratch_shapes=[
            pltpu.VMEM((NY, BLK, orbitals), jnp.float32),
            pltpu.VMEM((NY * BLK, orbitals), jnp.bfloat16),
            pltpu.VMEM((NY * BLK, orbitals), jnp.bfloat16),
            pltpu.VMEM((times, NX * NC, NZ, NY, 32, BLK), jnp.float32),
            pltpu.VMEM((times, NX * NC, NZ, NY, 32, BLK), jnp.float32),
            pltpu.VMEM((times, NZ, NY, BLK, BLK), jnp.float32),
            pltpu.VMEM((times, NZ, NY, BLK, BLK), jnp.float32),
            pltpu.VMEM((orbitals, 2 * BLK), jnp.bfloat16),
            pltpu.VMEM((orbitals, 2 * BLK), jnp.bfloat16),
            pltpu.VMEM((2 * BLK, NY * BLK), jnp.bfloat16),
            pltpu.VMEM((2 * BLK, NY * BLK), jnp.bfloat16),
            dma(()),
            dma((2, 2)),
            dma((2, 2)),
            dma((2, 2)),
            dma((2, 2)),
            dma((2, 2)),
            dma((2, 2)),
            dma((2, 2, 2)),
            dma((2, 2)),
            dma((2, 2)),
            dma((2, 2)),
            dma((2, 2)),
            dma((2,)),
            dma((2, NX)),
        ],
        compiler_params=pltpu.CompilerParams(
            collective_id=0, has_side_effects=True, vmem_limit_bytes=60 * 2**20
        ),
        name="contract",
    )(mask, three_center, occ_density, vir_density)
    return coupled[:, :, None]


def solution(mesh):
    in_specs = (
        P("aux", "orb", None, None),
        P(None, "aux", None, None),
        P(None, "orb", "aux"),
        P(None, "orb", "aux"),
    )
    out_specs = P(None, "aux", "orb", None, None)
    return jax.shard_map(local, mesh=mesh, in_specs=in_specs, out_specs=out_specs, check_vma=False)
```

time: 403 us -> 153 us (0.38); the launches traced: 396 us -> 153 us
  waiting for transfers between devices: 270 us -> 0 us
  Pallas kernels: 0 us -> 147 us
  matrix products: 38.4 us -> 0 us
  blocking collectives: 27.1 us -> 0 us
  local copies, waits for them, and re-layouts: 28.7 us -> 6.02 us
  starting transfers between devices: 16 us -> 0 us
  between operations: 13.2 us -> 0.01 us
    all_gather x4 -> x0, waiting for transfers between devices: 215 us -> none  [the longest x2 135 us: local(): lax.all_gather(occ_cols[moment:moment + 1], 'orb', axis=1, tiled=True)]
    pallas_call x0 -> x1, Pallas kernels: none -> 147 us  [local(): pl.pallas_call(kernel, out_shape=jax.ShapeDtypeStruct((times, NY, orbital...]
    all_to_all x2 -> x0, waiting for transfers between devices: 53.7 us -> none  [local(): lax.all_to_all(sending, 'orb', split_axis=0, concat_axis=0, tiled=True)]
    dot_general x4 -> x0, matrix products: 38.4 us -> none  [the longest x2 19.5 us: make_applier(): jnp.einsum('tsk,takl->tasl', density_rows, column_data, precision=lax.Pre...]
    all_gather x2 -> x0, blocking collectives: 27.1 us -> none  [the longest x1 14 us: local(): lax.all_gather(occ_density, 'aux', axis=2, tiled=True)]
    all_to_all x2 -> x0, starting transfers between devices: 15.9 us -> none  [local(): lax.all_to_all(sending, 'orb', split_axis=0, concat_axis=0, tiled=True)]
    dot_general x2 -> x0, local copies, waits for them, and re-layouts: 10.7 us -> none  [make_adder(): jnp.einsum('tar,trl->tal', masked, density_rows, precision=lax.Precision....]
    transpose x4 -> x0, local copies, waits for them, and re-layouts: 6.82 us -> none  [the longest x2 3.85 us: arrange(): reordered = grouped.transpose(2, 1, 3, 0, 4, 5)]
  transfers between devices with their start and end apart: 6 -> 0, of which waited for: 5 -> 0; matrix products, arithmetic and copies ran while one was open for 13% -> 0% of each run, Pallas kernels for 0% -> 0%
where the time goes in v1:
time: 153 us
  Pallas kernels  147 us (96%)
  local copies, waits for them, and re-layouts  6.02 us (4%)
    pallas_call x1, Pallas kernels, local(): pl.pallas_call(kernel, out_shape=jax.ShapeDtypeStruct((times, NY, orbital...  147 us
    unnamed x3, local copies, waits for them, and re-layouts  5.26 us

profile of v1, /device:TPU:57, one launch (start us, length us, event | category | flops | bytes accessed | tf_op | source)
XLA Modules:
  0.0 152.7 jit_solution(17538786071662035249)
XLA Ops:
  0.0 0.0 copy-start
  0.0 0.8 copy-done
  0.8 0.1 convert_reduce_fusion
  0.9 0.1 broadcast_in_dim.12
  0.9 0.7 broadcast_in_dim.13.mask
  1.6 146.6 %contract.1 = f32[2,4,1024,128]{3,2,1,0:T(8,128)} custom-call(f32[16,128]{1,0:T(8,128)} %broadcast_in_dim.13.mask, f32[4,1,128,1024]{3,2,1,0:T(8,128)} %three_center.1, f32[2,32,128]{2,1,0:T(8,128)} %occ_in.1, f32[2,32,128]{2,1,0:T(8,128)} %vir_in.1), custom_call_target="tpu_custom_call" | custom-call | tf_op jit(solution)/shard_map/contract/pallas_call | solution.py:258
  148.2 4.5 %copy.8 = f32[2,4,1,1024,128]{4,3,2,1,0:T(8,128)} copy(f32[2,4,1,1024,128]{4,3,2,1,0:T(8,128)} %bitcast.4) | data formatting | bytes 8388608
  (1 shorter events, 0.0 us)
Async XLA Ops:
  0.0 0.8 copy-start

commit v2 on v1

v2 whole, which is shorter than its diff:
```python
import functools

import jax
import jax.numpy as jnp
from jax import lax
from jax.experimental import pallas as pl
from jax.experimental.pallas import tpu as pltpu
from jax.sharding import PartitionSpec as P

MESH = pl.DeviceIdType.MESH
NX, NC, NZ, NY = 4, 2, 8, 4
BLK = 128
OCC, VIR = 0, 1


def split(value):
    high = value.astype(jnp.bfloat16)
    return high, (value - high.astype(jnp.float32)).astype(jnp.bfloat16)


def three_pass(a_high, a_low, b_high, b_low):
    dot = functools.partial(jnp.dot, preferred_element_type=jnp.float32)
    return dot(a_high, b_high) + dot(a_high, b_low) + dot(a_low, b_high)


def kernel(
    tile_lists, three_center, occ_in, vir_in, coupled,
    lists, mask, rows, int_high, int_low, occ, vir, sending, received,
    one_high, one_low, two_high, two_low,
    rows_sem, own_sem, zs, zr, ys, yr, xs, xr, rs, rr, cs, cr, out_sem, in_sem,
    x0s, x0r, z0s, z0r, y0s, y0r, r0s, r0r, c0s, c0r,
):
    aux, orb = lax.axis_index("aux"), lax.axis_index("orb")
    x, c, z, y = lax.div(aux, NC), lax.rem(aux, NC), lax.div(orb, NY), lax.rem(orb, NY)
    pair = lax.div(z, 2)
    inputs, full = (occ_in, vir_in), (occ, vir)

    def device(at_x, at_c, at_z, at_y):
        return (at_x * NC + at_c, at_z * NY + at_y)

    def along_x(step):
        return lax.rem(x + step + NX, NX)

    def along_z(step):
        return lax.rem(z + step, NZ)

    def along_y(step):
        return lax.rem(y + step, NY)

    def send(source, target, send_sem, recv_sem, to):
        pltpu.make_async_remote_copy(
            src_ref=source, dst_ref=target, send_sem=send_sem, recv_sem=recv_sem,
            device_id=to, device_id_type=MESH,
        ).start()

    def wait(ref, sem):
        pltpu.make_async_copy(ref, ref, sem).wait()

    def own_copy(g, t):
        return pltpu.make_async_copy(inputs[g].at[t], full[g].at[t, x, c, z, y], own_sem.at[g, t])

    rows_copy = pltpu.make_async_copy(three_center.at[:, 0], rows, rows_sem.at[0])
    lists_copy = pltpu.make_async_copy(tile_lists.at[:, y], lists, rows_sem.at[1])
    for g in (OCC, VIR):
        for t in range(2):
            own_copy(g, t).start()
    lists_copy.start()
    rows_copy.start()

    barrier = pltpu.get_barrier_semaphore()
    peers = [device(x, c, along_z(d), y) for d in range(1, NZ)]
    peers += [device(x, c, z, along_y(d)) for d in range(1, NY)]
    peers += [device(along_x(d), c, z, y) for d in range(1, NX)]
    peers += [device(x, 1 - c, z, y)]
    for peer in peers:
        pl.semaphore_signal(barrier, inc=1, device_id=peer, device_id_type=MESH)
    pl.semaphore_wait(barrier, len(peers))

    def wanted(at_z, k):
        return lax.rem(lax.div(at_z, 2) + 2 + k, NX)

    def first_x_start():
        own_copy(OCC, 0).wait()
        piece = occ.at[0, x, c, z, y]
        for d in (2, 1, 3):
            send(piece, piece, x0s, x0r, device(along_x(d), c, z, y))

    def first_z_start():
        wait(occ.at[0, pl.ds(0, NX - 1), c, z, y], x0r)
        for k in range(NX):
            for d in (4, 3, 5, 2, 6, 1, 7):
                at_z = along_z(d)
                piece = occ.at[0, wanted(at_z, k), c, z, y]
                send(piece, piece, z0s, z0r.at[k], device(x, c, at_z, y))

    def first_y_start(k):
        wait(occ.at[0, 0, c, pl.ds(0, NZ - 1), y], z0r.at[k])
        piece = occ.at[0, wanted(z, k), c, :, y]
        for side, step in enumerate((1, 3)):
            send(piece, piece, y0s, y0r.at[k, side], device(x, c, z, along_y(step)))

    def first_y_relay(k):
        for side, (origin, onward) in enumerate(((3, 1), (1, 3))):
            from_y, to_y = along_y(origin), along_y(onward)
            wait(occ.at[0, 0, c, :, from_y], y0r.at[k, side])
            piece = occ.at[0, wanted(z, k), c, pl.ds(side * (NZ // 2), NZ // 2), from_y]
            send(piece, piece, r0s, r0r.at[k], device(x, c, z, to_y))

    def first_finish(k):
        wait(occ.at[0, 0, c, :, y], r0r.at[k])
        piece = occ.at[0, wanted(z, k), c]
        send(piece, piece, c0s, c0r.at[k], device(x, 1 - c, z, y))
        wait(piece, c0r.at[k])

    def z_start(g, t):
        own_copy(g, t).wait()
        piece = full[g].at[t, x, c, z, y]
        for d in (4, 3, 5, 2, 6, 1, 7):
            send(piece, piece, zs.at[g, t], zr.at[g, t], device(x, c, along_z(d), y))

    def z_wait(g, t):
        wait(full[g].at[t, x, c, pl.ds(0, NZ - 1), y], zr.at[g, t])

    def y_start(g, t):
        piece = full[g].at[t, x, c, :, y]
        for d in (2, 1, 3):
            send(piece, piece, ys.at[g, t], yr.at[g, t], device(x, c, z, along_y(d)))

    def y_wait(g, t):
        wait(full[g].at[t, x, c, :, pl.ds(0, NY - 1)], yr.at[g, t])

    def column(g, t, at_x):
        return full[g].at[t, at_x, c]

    def core_start(g, t, at_x):
        piece = column(g, t, at_x)
        send(piece, piece, cs.at[g, t], cr.at[g, t], device(x, 1 - c, z, y))

    def core_wait(g, t):
        wait(full[g].at[t, :, c], cr.at[g, t])

    def x_start(g, t):
        piece = column(g, t, x)
        send(piece, piece, xs.at[g, t], xr.at[g, t, 0], device(along_x(1), c, z, y))
        send(piece, piece, xs.at[g, t], xr.at[g, t, 1], device(along_x(-1), c, z, y))
        core_start(g, t, x)

    def x_relay(g, t):
        for side, (origin, onward) in enumerate(((-1, 1), (1, -1))):
            at_x = along_x(origin)
            wait(column(g, t, at_x), xr.at[g, t, side])
            piece = full[g].at[t, at_x, c, pl.ds(side * (NZ // 2), NZ // 2)]
            send(piece, piece, rs.at[g, t], rr.at[g, t], device(along_x(onward), c, z, y))
            core_start(g, t, at_x)

    def x_finish(g, t):
        at_x = along_x(2)
        wait(column(g, t, at_x), rr.at[g, t])
        core_start(g, t, at_x)

    def make_mask():
        lists_copy.wait()
        numbers = lax.broadcasted_iota(jnp.int32, (NZ, NZ), 0)
        for t in range(2):
            matches = (lists[t, pl.ds(z, 1), :] == numbers).astype(jnp.float32)
            total = jnp.sum(matches, axis=1, keepdims=True)
            mask[pl.ds(t * NZ, NZ), :] = jnp.broadcast_to(total, (NZ, BLK))

    def half_unit(t, k):
        p = wanted(z, k)
        for h in range(2):
            for n in range(NZ):
                block = occ[t, p, h, n].reshape(BLK, BLK)
                block = block * mask[pl.ds(t * NZ + n, 1), :]
                high, low = split(block)
                one_high[pl.ds(n * BLK, BLK), pl.ds(h * BLK, BLK)] = high
                one_low[pl.ds(n * BLK, BLK), pl.ds(h * BLK, BLK)] = low
        product = three_pass(int_high[...], int_low[...], one_high[...], one_low[...])
        for h in range(2):
            keep = mask[pl.ds(t * NZ + 2 * p + h, 1), :]
            for r in range(NY):
                part = product[r * BLK : (r + 1) * BLK, h * BLK : (h + 1) * BLK]
                sending[t, 2 * p + h, r] = part * keep
        for d in (2, 1, 3):
            to_y = along_y(d)
            for h in range(2):
                to_z = 2 * p + h
                send(
                    sending.at[t, to_z, to_y], received.at[t, z, y],
                    out_sem.at[t], in_sem.at[t, pair], device(x, c, to_z, to_y),
                )
        for h in range(2):
            to_z = 2 * p + h
            source, target = sending.at[t, to_z, y], received.at[t, z, y]

            @pl.when(to_z == z)
            def _():
                pltpu.make_async_copy(source, target, in_sem.at[t, pair]).start()

            @pl.when(to_z != z)
            def _():
                send(source, target, out_sem.at[t], in_sem.at[t, pair], device(x, c, to_z, y))

    def half_stage(t):
        def unit(k, carry):
            half_unit(t, k)
            return carry

        lax.fori_loop(0, NX, unit, 0)

    def full_stage(t):
        def unit(k, carry):
            p = lax.rem(pair + 2 - k + NX, NX)
            wait(received.at[t, pl.ds(2 * p, 2)], in_sem.at[t, p])
            for h in range(2):
                for q in range(NY):
                    high, low = split(received[t, 2 * p + h, q])
                    two_high[pl.ds(h * BLK, BLK), pl.ds(q * BLK, BLK)] = high
                    two_low[pl.ds(h * BLK, BLK), pl.ds(q * BLK, BLK)] = low

            def tile(s, inner):
                halves = [
                    split(vir[t, p, h, pl.ds(2 * s, 2)].reshape(2 * BLK, BLK))
                    for h in range(2)
                ]
                high = jnp.concatenate([halves[0][0], halves[1][0]], axis=1)
                low = jnp.concatenate([halves[0][1], halves[1][1]], axis=1)
                product = three_pass(high, low, two_high[...], two_low[...])
                for q in range(NY):
                    at = (t, q, pl.ds(s * 2 * BLK, 2 * BLK), slice(None))
                    coupled[at] += product[:, q * BLK : (q + 1) * BLK]
                return inner

            lax.fori_loop(0, NZ // 2, tile, 0)
            return carry

        lax.fori_loop(0, NX, unit, 0)

    first_x_start()
    z_start(OCC, 1)
    first_z_start()
    z_start(VIR, 0)
    z_start(VIR, 1)
    rows_copy.wait()
    for r in range(NY):
        high, low = split(rows[r])
        int_high[pl.ds(r * BLK, BLK), :] = high
        int_low[pl.ds(r * BLK, BLK), :] = low
    make_mask()
    coupled[...] = jnp.zeros_like(coupled)

    def first_unit(k):
        first_finish(k)
        half_unit(0, k)

    first_y_start(0)
    first_y_start(1)
    first_y_relay(0)
    first_y_start(2)
    first_y_relay(1)
    first_y_start(3)
    z_wait(OCC, 1)
    y_start(OCC, 1)
    first_unit(0)
    first_y_relay(2)
    first_unit(1)
    first_y_relay(3)
    y_wait(OCC, 1)
    x_start(OCC, 1)
    for t in range(2):
        z_wait(VIR, t)
        y_start(VIR, t)
    first_unit(2)
    first_unit(3)
    x_relay(OCC, 1)
    y_wait(VIR, 0)
    x_start(VIR, 0)
    x_finish(OCC, 1)
    core_wait(OCC, 1)
    half_stage(1)
    x_relay(VIR, 0)
    y_wait(VIR, 1)
    x_start(VIR, 1)
    x_finish(VIR, 0)
    core_wait(VIR, 0)
    x_relay(VIR, 1)
    x_finish(VIR, 1)
    core_wait(VIR, 1)
    full_stage(0)
    full_stage(1)

    wait(occ.at[0, pl.ds(0, NX - 1), c, z, y], x0s)
    wait(occ.at[0, :, c, pl.ds(0, NZ - 1), y], z0s)
    wait(occ.at[0, :, c, :, pl.ds(0, 2)], y0s)
    wait(occ.at[0, :, c, :, 0], r0s)
    wait(occ.at[0, :, c], c0s)
    for g, t in ((OCC, 1), (VIR, 0), (VIR, 1)):
        wait(full[g].at[t, x, c, pl.ds(0, NZ - 1), y], zs.at[g, t])
        wait(full[g].at[t, x, c, :, pl.ds(0, NY - 1)], ys.at[g, t])
        wait(full[g].at[t, pl.ds(0, 2), c], xs.at[g, t])
        wait(full[g].at[t, 0, c], rs.at[g, t])
        wait(full[g].at[t, :, c], cs.at[g, t])
    for t in range(2):
        wait(sending.at[t, pl.ds(0, NZ - 1)], out_sem.at[t])
        wait(sending.at[t, 0, pl.ds(0, NY - 1)], out_sem.at[t])


def local(three_center, tile_lists, occ_density, vir_density):
    times, blocks = tile_lists.shape[0], tile_lists.shape[3]
    orbitals = three_center.shape[3]
    dma = pltpu.SemaphoreType.DMA
    coupled = pl.pallas_call(
        kernel,
        out_shape=pltpu.VMEM((times, NY, orbitals, BLK), jnp.float32),
        in_specs=[pl.BlockSpec(memory_space=pltpu.HBM)] * 4,
        out_specs=pl.BlockSpec(memory_space=pltpu.VMEM),
        scratch_shapes=[
            pltpu.VMEM((times, blocks, blocks), jnp.int32),
            pltpu.VMEM((times * blocks, BLK), jnp.float32),
            pltpu.VMEM((NY, BLK, orbitals), jnp.float32),
            pltpu.VMEM((NY * BLK, orbitals), jnp.bfloat16),
            pltpu.VMEM((NY * BLK, orbitals), jnp.bfloat16),
            pltpu.VMEM((times, NX, NC, NZ, NY, 32, BLK), jnp.float32),
            pltpu.VMEM((times, NX, NC, NZ, NY, 32, BLK), jnp.float32),
            pltpu.VMEM((times, NZ, NY, BLK, BLK), jnp.float32),
            pltpu.VMEM((times, NZ, NY, BLK, BLK), jnp.float32),
            pltpu.VMEM((orbitals, 2 * BLK), jnp.bfloat16),
            pltpu.VMEM((orbitals, 2 * BLK), jnp.bfloat16),
            pltpu.VMEM((2 * BLK, NY * BLK), jnp.bfloat16),
            pltpu.VMEM((2 * BLK, NY * BLK), jnp.bfloat16),
            dma((2,)),
            dma((2, 2)),
            dma((2, 2)),
            dma((2, 2)),
            dma((2, 2)),
            dma((2, 2)),
            dma((2, 2)),
            dma((2, 2, 2)),
            dma((2, 2)),
            dma((2, 2)),
            dma((2, 2)),
            dma((2, 2)),
            dma((2,)),
            dma((2, NX)),
            dma(()),
            dma(()),
            dma(()),
            dma((NX,)),
            dma(()),
            dma((NX, 2)),
            dma(()),
            dma((NX,)),
            dma(()),
            dma((NX,)),
        ],
        compiler_params=pltpu.CompilerParams(
            collective_id=0, has_side_effects=True, vmem_limit_bytes=36 * 2**20
        ),
        name="contract",
    )(*(pltpu.with_memory_space_constraint(a, pltpu.HBM) for a in (tile_lists, three_center, occ_density, vir_density)))
    return coupled[:, :, None]


def solution(mesh):
    in_specs = (
        P("aux", "orb", None, None),
        P(None, "aux", None, None),
        P(None, "orb", "aux"),
        P(None, "orb", "aux"),
    )
    out_specs = P(None, "aux", "orb", None, None)
    return jax.shard_map(local, mesh=mesh, in_specs=in_specs, out_specs=out_specs, check_vma=False)
```

time: 153 us -> 134 us (0.88)
  the two profiles are of different devices: /device:TPU:57 before, /device:TPU:123 now
where the time goes in v2:
time: 134 us; the launch traced here: 133 us
  Pallas kernels  131 us (98%)
  local copies, waits for them, and re-layouts  2.02 us (2%)
    pallas_call x1, Pallas kernels, local(): pl.pallas_call(kernel, out_shape=pltpu.VMEM((times, NY, orbitals, BLK), j...  131 us

profile of v2, /device:TPU:123, one launch (start us, length us, event | category | flops | bytes accessed | tf_op | source)
XLA Modules:
  0.0 133.5 jit_solution(10317886513535007476)
XLA Ops:
  0.0 131.4 %contract.1 = f32[2,4,1024,128]{3,2,1,0:T(8,128)S(1)} custom-call(s32[2,4,8,8]{3,2,1,0:T(8,128)} %tile_lists.1, f32[4,1,128,1024]{3,2,1,0:T(8,128)} %three_center.1, f32[2,32,128]{2,1,0:T(8,128)} %occ_in.1, f32[2,32,128]{2,1,0:T(8,128)} %vir_in.1), custom_call_target="tpu_custom_call" | custom-call | tf_op jit(solution)/shard_map/contract/pallas_call | solution.py:312
  131.4 2.0 %copy.7 = f32[2,4,1,1024,128]{4,3,2,1,0:T(8,128)} copy(f32[2,4,1,1024,128]{4,3,2,1,0:T(8,128)S(1)} %bitcast.3) | data formatting | bytes 8388608

commit v3 on v2

--- a/solution.py
+++ b/solution.py
@@ -267,11 +267,12 @@
     first_y_relay(3)
     y_wait(OCC, 1)
     x_start(OCC, 1)
-    for t in range(2):
-        z_wait(VIR, t)
-        y_start(VIR, t)
     first_unit(2)
     first_unit(3)
+    z_wait(VIR, 0)
+    y_start(VIR, 0)
+    z_wait(VIR, 1)
+    y_start(VIR, 1)
     x_relay(OCC, 1)
     y_wait(VIR, 0)
     x_start(VIR, 0)

time: 134 us -> 132 us (0.985)
  the two profiles are of different devices: /device:TPU:123 before, /device:TPU:57 now
where the time goes in v3:
time: 132 us; the launch traced here: 130 us
  Pallas kernels  127 us (96%)
  local copies, waits for them, and re-layouts  2.02 us (2%)
    pallas_call x1, Pallas kernels, local(): pl.pallas_call(kernel, out_shape=pltpu.VMEM((times, NY, orbitals, BLK), j...  127 us

profile of v3, /device:TPU:57, one launch (start us, length us, event | category | flops | bytes accessed | tf_op | source)
XLA Modules:
  0.0 129.5 jit_solution(14021169957340997132)
XLA Ops:
  0.0 127.5 %contract.1 = f32[2,4,1024,128]{3,2,1,0:T(8,128)S(1)} custom-call(s32[2,4,8,8]{3,2,1,0:T(8,128)} %tile_lists.1, f32[4,1,128,1024]{3,2,1,0:T(8,128)} %three_center.1, f32[2,32,128]{2,1,0:T(8,128)} %occ_in.1, f32[2,32,128]{2,1,0:T(8,128)} %vir_in.1), custom_call_target="tpu_custom_call" | custom-call | tf_op jit(solution)/shard_map/contract/pallas_call | solution.py:313
  127.5 2.0 %copy.7 = f32[2,4,1,1024,128]{4,3,2,1,0:T(8,128)} copy(f32[2,4,1,1024,128]{4,3,2,1,0:T(8,128)S(1)} %bitcast.3) | data formatting | bytes 8388608
